TPU v7x, 256 devices: a whole 4x4x8 slice. The times are simulated.
256 devices in a mesh: row: 2 (over core), col: 8 (over z), cuts: 16 (over y, x).
Axes of the slice: x: 4, y: 4, z: 8, core: 2. Of those that a mesh axis runs over, the one named last changes fastest.
Arguments:
- y_blocks: bfloat16 [128, 12, 128, 128], P('cuts', None, ('row', 'col')), may hold values from -0.5 to 0.5
- z_blocks: bfloat16 [128, 12, 128, 128], P('cuts', None, ('row', 'col')), may hold values from -0.59765625 to 0.59765625
- pattern: int32 [128, 12], replicated, may hold values from 0 to 127, as said below
Outputs:
- z_next: bfloat16 [128, 12, 128, 128], P('cuts', None, ('row', 'col'))
Inputs may be any that keep to these rules, and one draw needn't show every extreme that they name: `pattern`: row i lists 12 distinct block columns, i among them, each equal to i + d modulo 128 for some d with -6 <= d <= 6.
All inputs are finite; a program needn't handle non-finite values.
Results may differ from a plain program's by a relative error of at most 0.0049.
Values may be sent and summed in bfloat16 or wider, within the bound.
A program may use at most 64 MiB of HBM per device.

v0:
```python
import jax
import jax.numpy as jnp
from jax import lax
from jax.sharding import PartitionSpec as P

HALO = 6


def extended(cells, sides, width):
    for axis, dim in sides:
        count = lax.axis_size(axis)
        head = lax.slice_in_dim(cells, 0, width, axis=dim)
        tail = lax.slice_in_dim(cells, cells.shape[dim] - width, cells.shape[dim], axis=dim)
        cells = jnp.concatenate(
            [
                lax.ppermute(tail, axis, [(i, (i + 1) % count) for i in range(count)]),
                cells,
                lax.ppermute(head, axis, [((i + 1) % count, i) for i in range(count)]),
            ],
            axis=dim,
        )
    return cells


def pattern_tables(pattern, row_first, row_count):
    total_rows = pattern.shape[0]
    own_cols = lax.dynamic_slice_in_dim(pattern, row_first, row_count, 0)
    row_numbers = row_first + jnp.arange(row_count, dtype=jnp.int32)
    distance = (own_cols - row_numbers[:, None] + HALO) % total_rows - HALO
    padded = jnp.concatenate([pattern[total_rows - HALO :], pattern, pattern[:HALO]], axis=0)
    window_cols = lax.dynamic_slice_in_dim(padded, row_first, row_count + 2 * HALO, 0)
    selectors = []
    matchings = []
    for offset in range(2 * HALO + 1):
        selectors.append((distance == offset - HALO).astype(jnp.bfloat16))
        near_cols = window_cols[offset : offset + row_count]
        matchings.append((near_cols[:, :, None] == own_cols[:, None, :]).astype(jnp.float32))
    return (jnp.stack(selectors), jnp.stack(matchings), own_cols, row_numbers)


def select_left(left_blocks, selectors):
    chosen = jnp.einsum(
        "dim,imab->diab", selectors, left_blocks, preferred_element_type=jnp.float32
    )
    return chosen.astype(jnp.bfloat16)


def make_folder(chosen, matchings, row_count, running, segment):

    def step(offset, partial_value):
        near_rows = lax.dynamic_slice_in_dim(segment, offset, row_count, 0)
        left_rows = lax.dynamic_index_in_dim(chosen, offset, 0, keepdims=False)
        matching = lax.dynamic_index_in_dim(matchings, offset, 0, keepdims=False)
        products = jnp.einsum(
            "iab,inbe->inae", left_rows, near_rows, preferred_element_type=jnp.float32
        )
        summed = partial_value
        for slot in range(products.shape[1]):
            summed = summed + matching[:, slot, :, None, None] * products[:, slot][:, None]
        return summed

    return lax.fori_loop(0, chosen.shape[0], step, running)


def local(y_blocks, z_blocks, pattern):
    row_count, slot_count, part_rows, block_width = y_blocks.shape
    row_first = lax.axis_index("cuts") * row_count
    selectors, matchings, own_cols, row_numbers = pattern_tables(pattern, row_first, row_count)
    zero_sum = jnp.zeros(y_blocks.shape, jnp.float32)
    z_window = extended(z_blocks, (("cuts", 0),), HALO)
    y_chosen = select_left(y_blocks, selectors)
    product = make_folder(
        y_chosen,
        matchings,
        row_count,
        zero_sum,
        lax.all_gather(z_window, ("row", "col"), axis=2, tiled=True),
    )
    a_first = (lax.axis_index("row") * lax.axis_size("col") + lax.axis_index("col")) * part_rows
    diagonal = (own_cols == row_numbers[:, None]).astype(jnp.float32)
    tile_rows = a_first + jnp.arange(part_rows, dtype=jnp.int32)
    tile_cols = jnp.arange(block_width, dtype=jnp.int32)
    eye_part = (tile_rows[:, None] == tile_cols[None, :]).astype(jnp.float32)
    q_blocks = (3.0 * diagonal[:, :, None, None] * eye_part[None, None] - product).astype(
        jnp.bfloat16
    )
    q_window = extended(q_blocks, (("cuts", 0),), HALO)
    z_chosen = select_left(z_blocks, selectors)
    second = make_folder(
        z_chosen,
        matchings,
        row_count,
        zero_sum,
        lax.all_gather(q_window, ("row", "col"), axis=2, tiled=True),
    )
    return (0.5 * second).astype(jnp.bfloat16)


def solution(mesh):
    return jax.shard_map(
        local,
        mesh=mesh,
        in_specs=(
            P("cuts", None, ("row", "col"), None),
            P("cuts", None, ("row", "col"), None),
            P(),
        ),
        out_specs=P("cuts", None, ("row", "col"), None),
        check_vma=False,
    )
```

profile of v0, /device:TPU:1, one launch (start us, length us, event | category | flops | bytes accessed | tf_op | source)
XLA Modules:
  0.0 270.0 jit_solution(11296862383216839759)
XLA Ops:
  9.7 3.8 %collective-permute-start.1 = (bf16[6,12,8,128]{3,2,1,0:T(8,128)(2,1)S(1)}, bf16[6,12,8,128]{3,2,1,0:T(8,128)(2,1)S(1)}, u32[]{:S(2)}, u32[]{:S(2)}) collective-permute-start(bf16[6,12,8,128]{3,2,1,0:T(8,128)(2,1)S(1)} %get-tuple-element.314), channel_id=1, source_target_pairs={{1,0},{2,1},{3,2},{4,3},{5,4},{6,5},{7,6},{8,7},{9,8},{10,9},{11,1... | collective-permute-start | bytes 442376 | tf_op jit(solution)/shard_map/ppermute | solution.py:18
  13.5 2.4 collective-permute-done
  22.6 63.0 %all-gather.3.cloned.1.call-done = bf16[20,12,128,128]{3,2,1,0:T(8,128)(2,1)} async-done(((bf16[20,12,8,128]{3,2,1,0:T(8,128)(2,1)}), bf16[20,12,128,128]{3,2,1,0:T(8,128)(2,1)}) %all-gather.3.cloned.1.call-update) | async-done | bytes 7864336 | tf_op jit(solution)/shard_map/all_gather | solution.py:77
  85.6 52.2 %while.28 = (s32[]{:T(128)}, f32[8,12,8,128]{3,2,1,0:T(8,128)S(1)}, f32[13,8,12,12]{3,1,2,0:T(8,128)S(1)}, bf16[20,12,128,128]{3,2,1,0:T(8,128)(2,1)}, bf16[13,8...) while((s32[]{:T(128)}, f32[8,12,8,128]{3,2,1,0:T(8,128)S(1)}, ...), condition=%wide.region_1.2_spmd.clone, body=%wide.region_0.1_spmd.clone.sunk | while | flops 27623424 | bytes 5545563 | solution.py:62
  85.6 2.4 fusion.64
  89.6 2.4 fusion.64
  93.7 2.4 fusion.64
  97.7 2.4 fusion.64
  101.7 2.4 fusion.64
  105.7 2.4 fusion.64
  109.7 2.4 fusion.64
  113.7 2.4 fusion.64
  117.7 2.4 fusion.64
  121.8 2.4 fusion.64
  129.8 2.4 fusion.64
  133.8 2.4 fusion.64
  138.6 4.3 %collective-permute-start.3 = (bf16[6,12,8,128]{3,2,1,0:T(8,128)(2,1)S(1)}, bf16[6,12,8,128]{3,2,1,0:T(8,128)(2,1)S(1)}, u32[]{:S(2)}, u32[]{:S(2)}) collective-permute-start(bf16[6,12,8,128]{3,2,1,0:T(8,128)(2,1)S(1)} %get-tuple-element.312), channel_id=1, source_target_pairs={{1,0},{2,1},{3,2},{4,3},{5,4},{6,5},{7,6},{8,7},{9,8},{10,9},{11,1... | collective-permute-start | bytes 442376 | tf_op jit(solution)/shard_map/ppermute | solution.py:18
  142.9 3.7 %collective-permute-done.2 = bf16[6,12,8,128]{3,2,1,0:T(8,128)(2,1)S(1)} collective-permute-done((bf16[6,12,8,128]{3,2,1,0:T(8,128)(2,1)S(1)}, bf16[6,12,8,128]{3,2,1,0:T(8,128)(2,1)S(1)}, u32[]{:S(2)}, u32[]{:S(2)}) %collective-permute-start.2) | collective-permute-done | bytes 147488 | tf_op jit(solution)/shard_map/ppermute | solution.py:16
  147.8 62.5 %all-gather.5.cloned.1.call-done = bf16[20,12,128,128]{3,2,1,0:T(8,128)(2,1)} async-done(((bf16[20,12,8,128]{3,2,1,0:T(8,128)(2,1)}), bf16[20,12,128,128]{3,2,1,0:T(8,128)(2,1)}) %all-gather.5.cloned.1.call-update) | async-done | bytes 7864336 | tf_op jit(solution)/shard_map/all_gather | solution.py:94
  210.3 52.2 %while.29 = (s32[]{:T(128)}, f32[8,12,8,128]{3,2,1,0:T(8,128)S(1)}, f32[13,8,12,12]{3,1,2,0:T(8,128)S(1)}, bf16[20,12,128,128]{3,2,1,0:T(8,128)(2,1)}, bf16[13,8...) while((s32[]{:T(128)}, f32[8,12,8,128]{3,2,1,0:T(8,128)S(1)}, ...), condition=%wide.region_3.4_spmd.clone, body=%wide.region_2.3_spmd.clone.sunk | while | flops 27623424 | bytes 5545563 | solution.py:62
  226.3 2.4 fusion.68
  230.4 2.4 fusion.68
  246.4 2.4 fusion.68
  250.4 2.4 fusion.68
  (177 shorter events, 76.8 us)
Async XLA Ops:
  6.5 15.6 %copy-start = (bf16[8,12,8,128]{3,2,1,0:T(8,128)(2,1)S(1)}, bf16[8,12,8,128]{3,2,1,0:T(8,128)(2,1)}, u32[]{:S(2)}) copy-start(bf16[8,12,8,128]{3,2,1,0:T(8,128)(2,1)} %param.7) | copy-start | bytes 589828
  6.5 79.0 %all-gather.3.cloned.1.call-start = ((), (), s32[]{:S(2)}) async-start(), calls=%async_computation | async-start | bytes 8355840 | tf_op jit(solution)/shard_map/all_gather | solution.py:77
  7.6 8.4 %collective-permute-start = (bf16[6,12,8,128]{3,2,1,0:T(8,128)(2,1)S(1)}, bf16[6,12,8,128]{3,2,1,0:T(8,128)(2,1)S(1)}, u32[]{:S(2)}, u32[]{:S(2)}) collective-permute-start(bf16[6,12,8,128]{3,2,1,0:T(8,128)(2,1)S(1)} %get-tuple-element.313), channel_id=1, source_target_pairs={{0,1},{1,2},{2,3},{3,4},{4,5},{5,6},{6,7},{7,8},{8,9},{9,10},{10,1... | collective-permute-start | bytes 442376 | tf_op jit(solution)/shard_map/ppermute | solution.py:16
  9.7 6.3 %collective-permute-start.1 = (bf16[6,12,8,128]{3,2,1,0:T(8,128)(2,1)S(1)}, bf16[6,12,8,128]{3,2,1,0:T(8,128)(2,1)S(1)}, u32[]{:S(2)}, u32[]{:S(2)}) collective-permute-start(bf16[6,12,8,128]{3,2,1,0:T(8,128)(2,1)S(1)} %get-tuple-element.314), channel_id=1, source_target_pairs={{1,0},{2,1},{3,2},{4,3},{5,4},{6,5},{7,6},{8,7},{9,8},{10,9},{11,1... | collective-permute-start | bytes 442376 | tf_op jit(solution)/shard_map/ppermute | solution.py:18
  17.8 192.5 %all-gather.5.cloned.1.call-start = ((), (), s32[]{:S(2)}) async-start(), calls=%async_computation.1 | async-start | bytes 8355840 | tf_op jit(solution)/shard_map/all_gather | solution.py:94
  85.6 61.9 %copy-start.1 = (bf16[8,12,8,128]{3,2,1,0:T(8,128)(2,1)S(1)}, bf16[8,12,8,128]{3,2,1,0:T(8,128)(2,1)}, u32[]{:S(2)}) copy-start(bf16[8,12,8,128]{3,2,1,0:T(8,128)(2,1)} %param.8) | copy-start | bytes 589828
  138.0 8.5 %collective-permute-start.2 = (bf16[6,12,8,128]{3,2,1,0:T(8,128)(2,1)S(1)}, bf16[6,12,8,128]{3,2,1,0:T(8,128)(2,1)S(1)}, u32[]{:S(2)}, u32[]{:S(2)}) collective-permute-start(bf16[6,12,8,128]{3,2,1,0:T(8,128)(2,1)S(1)} %get-tuple-element.311), channel_id=1, source_target_pairs={{0,1},{1,2},{2,3},{3,4},{4,5},{5,6},{6,7},{7,8},{8,9},{9,10},{10,1... | collective-permute-start | bytes 442376 | tf_op jit(solution)/shard_map/ppermute | solution.py:16
  138.6 7.9 %collective-permute-start.3 = (bf16[6,12,8,128]{3,2,1,0:T(8,128)(2,1)S(1)}, bf16[6,12,8,128]{3,2,1,0:T(8,128)(2,1)S(1)}, u32[]{:S(2)}, u32[]{:S(2)}) collective-permute-start(bf16[6,12,8,128]{3,2,1,0:T(8,128)(2,1)S(1)} %get-tuple-element.312), channel_id=1, source_target_pairs={{1,0},{2,1},{3,2},{4,3},{5,4},{6,5},{7,6},{8,7},{9,8},{10,9},{11,1... | collective-permute-start | bytes 442376 | tf_op jit(solution)/shard_map/ppermute | solution.py:18
Sparse Core Ops, SparseCore 0:
  17.9 67.6 all-gather.2
  147.6 62.6 all-gather.4
where the time goes:
time: 271 us; the launch traced here: 270 us
  waiting for transfers between devices  132 us (49%)
  matrix products  63 us (23%)
  other arithmetic  44.7 us (16%)
  between operations  13.7 us (5%)
  starting transfers between devices  10.8 us (4%)
  local copies, waits for them, and re-layouts  4.75 us (2%)
    all_gather x1, waiting for transfers between devices, local(): lax.all_gather(z_window, ('row', 'col'), axis=2, tiled=True)  63 us
    dot_general x26, matrix products, step(): jnp.einsum('iab,inbe->inae', left_rows, near_rows, preferred_element_type...  62.6 us
    all_gather x1, waiting for transfers between devices, local(): lax.all_gather(q_window, ('row', 'col'), axis=2, tiled=True)  62.5 us
    add x26, other arithmetic, step(): summed + matching[:, slot, :, None, None] * products[:, slot][:, None]  38.9 us
    ppermute x2, starting transfers between devices, extended(): lax.ppermute(head, axis, [((i + 1) % count, i) for i in range(count)])  8.07 us
    ppermute x2, waiting for transfers between devices, extended(): lax.ppermute(tail, axis, [(i, (i + 1) % count) for i in range(count)])  6.12 us
  transfers between devices with their start and end apart: 6, of which 4 were waited for; matrix products, arithmetic and copies ran while one was open for 2% of the time, Pallas kernels for 0%

commit v1 on v0

v1 whole, which is shorter than its diff:
```python
import functools

import jax
import jax.numpy as jnp
from jax import lax
from jax.experimental import pallas as pl
from jax.experimental.pallas import tpu as pltpu
from jax.sharding import PartitionSpec as P

HALO = 6
REACH = 2 * HALO + 1
FOLD = 16
SPLIT = ("row", "col")


def halo_rows(rows):
    count = lax.axis_size("cuts")
    return jnp.concatenate(
        [
            lax.ppermute(rows[-HALO:], "cuts", [(i, (i + 1) % count) for i in range(count)]),
            rows,
            lax.ppermute(rows[:HALO], "cuts", [((i + 1) % count, i) for i in range(count)]),
        ],
        axis=0,
    )


def product_kernel(first, left_ref, right_ref, keep_ref, *rest):
    out_ref = rest[-1]
    i = pl.program_id(0)
    depth = left_ref.shape[2]
    block = depth // REACH
    right = right_ref[pl.ds(pl.multiple_of(i * block, block), depth), :]
    total = jnp.dot(left_ref[0], right, preferred_element_type=jnp.float32)
    kept = jnp.where(keep_ref[0] > 0, total, 0.0)
    half = kept.shape[1] // 2
    folded = kept[:, :half] + kept[:, half:]
    if first:
        diagonal_ref, eye_ref = rest[:2]
        folded = diagonal_ref[0] * eye_ref[...] - folded
    else:
        folded = 0.5 * folded
    out_ref[0] = folded.astype(out_ref.dtype)


def banded_product(left, right, keep, *diagonal):
    rows, block, depth = left.shape
    lanes = right.shape[1]
    specs = [
        pl.BlockSpec((1, block, depth), lambda i: (i, 0, 0)),
        pl.BlockSpec(right.shape, lambda i: (0, 0)),
        pl.BlockSpec((1, 1, lanes), lambda i: (i, 0, 0)),
    ]
    if diagonal:
        specs.append(pl.BlockSpec((1, 1, lanes // 2), lambda i: (i, 0, 0)))
        specs.append(pl.BlockSpec((block, lanes // 2), lambda i: (0, 0)))
    return pl.pallas_call(
        functools.partial(product_kernel, bool(diagonal)),
        grid=(rows,),
        in_specs=specs,
        out_specs=pl.BlockSpec((1, block, lanes // 2), lambda i: (i, 0, 0)),
        out_shape=jax.ShapeDtypeStruct((rows, block, lanes // 2), jnp.bfloat16),
        cost_estimate=pl.CostEstimate(
            flops=2 * rows * block * depth * lanes,
            bytes_accessed=2 * (left.size + right.size),
            transcendentals=0,
        ),
    )(left, right, keep, *diagonal)


def local(y_blocks, z_blocks, pattern):
    rows, slots, part, block = y_blocks.shape
    parts = block // part
    total_rows = pattern.shape[0]
    first_row = lax.axis_index("cuts") * rows
    me = lax.axis_index("row") * lax.axis_size("col") + lax.axis_index("col")
    own = lax.dynamic_slice_in_dim(pattern, first_row, rows, 0)
    row_numbers = first_row + jnp.arange(rows, dtype=jnp.int32)
    distance = (own - row_numbers[:, None] + HALO) % total_rows
    picks = (distance[:, :, None] == jnp.arange(REACH)[None, None, :]).astype(jnp.bfloat16)

    def dense(blocks):
        spread = jnp.einsum("imd,imab->diab", picks, blocks, preferred_element_type=jnp.float32)
        spread = spread.astype(jnp.bfloat16).transpose(1, 2, 0, 3)
        return spread.reshape(rows, part, REACH * block)

    z_left = lax.all_gather(dense(z_blocks), SPLIT, axis=1, tiled=True)
    y_left = lax.all_gather(dense(y_blocks), SPLIT, axis=1, tiled=True)

    lane = jnp.arange(FOLD * part, dtype=jnp.int32)
    lane_col, lane_in = lane // part, lane % part
    depth = jnp.arange(REACH * block, dtype=jnp.int32)
    depth_col = (row_numbers[:, None] + depth[None, :] // block - HALO) % FOLD
    chooser = (
        (depth_col[:, :, None] == lane_col[None, None, :])
        & ((depth % block)[None, :, None] == (me * part + lane_in)[None, None, :])
    ).astype(jnp.bfloat16)
    z_part = jnp.einsum(
        "iak,ikl->ial", z_left, chooser, preferred_element_type=jnp.float32
    ).astype(jnp.bfloat16)

    window = first_row - HALO + jnp.arange(rows + 2 * HALO, dtype=jnp.int32)
    start = window - HALO
    column = start[:, None] + (lane_col[None, :] - start[:, None]) % FOLD
    upper = (column // FOLD) % 2
    halves = jnp.concatenate([upper == 0, upper == 1], axis=1)

    def unfolded(folded):
        folded = halo_rows(folded)
        both = jnp.concatenate([folded, folded], axis=2)
        both = jnp.where(halves[:, None, :], both, jnp.zeros_like(both))
        return both.reshape((rows + 2 * HALO) * block, 2 * FOLD * part)

    wide_col = jnp.arange(2 * FOLD * part, dtype=jnp.int32) // part
    keep = jnp.any((own % (2 * FOLD))[:, :, None] == wide_col[None, None, :], axis=1)
    keep = keep.astype(jnp.float32)[:, None, :]
    diagonal = 3.0 * (row_numbers[:, None] % FOLD == lane_col[None, :]).astype(jnp.float32)
    inside = jnp.arange(block, dtype=jnp.int32)
    eye = (inside[:, None] == (me * part + lane_in)[None, :]).astype(jnp.float32)

    q_part = banded_product(y_left, unfolded(z_part), keep, diagonal[:, None, :], eye)
    next_part = banded_product(z_left, unfolded(q_part), keep)

    sent = next_part.reshape(rows, parts, part, FOLD * part).transpose(1, 0, 2, 3)
    got = lax.all_to_all(sent, SPLIT, 0, 0, tiled=True)
    got = got.reshape(parts, rows * part, FOLD * part)
    far = jnp.arange(FOLD * block, dtype=jnp.int32)
    mover = (
        (jnp.arange(parts)[:, None, None] == ((far % block) // part)[None, None, :])
        & (lane_col[None, :, None] == (far // block)[None, None, :])
        & (lane_in[None, :, None] == (far % part)[None, None, :])
    ).astype(jnp.bfloat16)
    moved = jnp.einsum("pml,pln->mn", got, mover, preferred_element_type=jnp.float32)
    moved = moved.astype(jnp.bfloat16).reshape(rows, part, FOLD, block)
    slot_pick = ((own % FOLD)[:, :, None] == jnp.arange(FOLD)[None, None, :]).astype(jnp.bfloat16)
    out = jnp.einsum("iqc,iace->iqae", slot_pick, moved, preferred_element_type=jnp.float32)
    return out.astype(jnp.bfloat16)


def solution(mesh):
    spec = P("cuts", None, SPLIT, None)
    return jax.shard_map(
        local, mesh=mesh, in_specs=(spec, spec, P()), out_specs=spec, check_vma=False
    )
```

time: 271 us -> 151 us (0.56)
  matrix products: 63 us -> 9.24 us
  waiting for transfers between devices: 132 us -> 84.5 us
  other arithmetic: 44.7 us -> 7.75 us
  Pallas kernels: 0 us -> 14.1 us
  starting transfers between devices: 10.8 us -> 15.4 us
    all_gather x2, waiting for transfers between devices: 125 us -> 66.6 us  [the longest x1 41 us: local(): z_left = lax.all_gather(dense(z_blocks), SPLIT, axis=1, tiled=True)]
    dot_general x28 -> x5, matrix products: 63 us -> 9.24 us  [the longest x1 4.54 us: local(): jnp.einsum('iak,ikl->ial', z_left, chooser, preferred_element_type=jnp.fl...]
    add x28 -> x2, other arithmetic: 39 us -> 0.01 us  [the longest x1 0.01 us: local(): me * part + lane_in]
    pallas_call x0 -> x2, Pallas kernels: none -> 14.1 us  [banded_product(): pl.pallas_call(functools.partial(product_kernel, bool(diagonal)), grid=(r...]
    all_to_all x0 -> x1, waiting for transfers between devices: none -> 9.2 us  [local(): got = lax.all_to_all(sent, SPLIT, 0, 0, tiled=True)]
    all_to_all x0 -> x1, starting transfers between devices: none -> 5.6 us  [local(): got = lax.all_to_all(sent, SPLIT, 0, 0, tiled=True)]
    select_n x0 -> x14, other arithmetic: none -> 4.46 us  [the longest x2 2.73 us: unfolded(): both = jnp.where(halves[:, None, :], both, jnp.zeros_like(both))]
  transfers between devices with their start and end apart: 6 -> 7, of which waited for: 4 -> 5; matrix products, arithmetic and copies ran while one was open for 2% -> 7% of each run, Pallas kernels for 0% -> 0%
where the time goes in v1:
time: 151 us
  waiting for transfers between devices  84.5 us (56%)
  starting transfers between devices  15.4 us (10%)
  Pallas kernels  14.1 us (9%)
  between operations  13.5 us (9%)
  matrix products  9.24 us (6%)
  other arithmetic  7.75 us (5%)
  local copies, waits for them, and re-layouts  6.01 us (4%)
    all_gather x1, waiting for transfers between devices, local(): z_left = lax.all_gather(dense(z_blocks), SPLIT, axis=1, tiled=True)  41 us
    all_gather x1, waiting for transfers between devices, local(): y_left = lax.all_gather(dense(y_blocks), SPLIT, axis=1, tiled=True)  25.6 us
    pallas_call x2, Pallas kernels, banded_product(): pl.pallas_call(functools.partial(product_kernel, bool(diagonal)), grid=(r...  14.1 us
    all_to_all x1, waiting for transfers between devices, local(): got = lax.all_to_all(sent, SPLIT, 0, 0, tiled=True)  9.2 us
    ppermute x2, waiting for transfers between devices, halo_rows(): lax.ppermute(rows[-HALO:], 'cuts', [(i, (i + 1) % count) for i in range(c...  8.74 us
    ppermute x2, starting transfers between devices, halo_rows(): lax.ppermute(rows[:HALO], 'cuts', [((i + 1) % count, i) for i in range(co...  7.21 us
    all_to_all x1, starting transfers between devices, local(): got = lax.all_to_all(sent, SPLIT, 0, 0, tiled=True)  5.6 us
    dot_general x1, matrix products, local(): jnp.einsum('iak,ikl->ial', z_left, chooser, preferred_element_type=jnp.fl...  4.54 us
  transfers between devices with their start and end apart: 7, of which 5 were waited for; matrix products, arithmetic and copies ran while one was open for 7% of the time, Pallas kernels for 0%

profile of v1, /device:TPU:1, one launch (start us, length us, event | category | flops | bytes accessed | tf_op | source)
XLA Modules:
  0.0 150.6 jit_solution(1958255381104384757)
XLA Ops:
  6.5 0.8 add_select_fusion.11
  7.4 0.8 add_select_fusion.8
  8.4 0.9 reshape.436
  9.4 1.1 fusion.17
  10.5 0.9 reshape.437
  13.4 41.0 %all-gather.3.cloned.1.call-done.left_ref = bf16[8,128,1664]{2,1,0:T(8,128)(2,1)} async-done(((bf16[8,8,1664]{2,1,0:T(8,128)(2,1)}), bf16[8,128,1664]{2,1,0:T(8,128)(2,1)}) %all-gather.3.cloned.1.call-update) | async-done | bytes 3407888 | tf_op jit(solution)/shard_map/all_gather | solution.py:87
  54.3 4.5 %fusion.12 = bf16[8,128,128]{2,1,0:T(8,128)(2,1)S(1)} fusion(bf16[8,128,1664]{2,1,0:T(8,128)(2,1)} %all-gather.3.cloned.1.call-done.left_ref, s32[128]{0:T(128)S(1)} %and_select_fusion.3, s32[8,1664]{1,0:T(8,128)S(1)} %add_select_fusion, pred[1664,128]{1,0:T(8,128)(4,1)S(1)} %broadcast_compare_fusion.2), kind=kOutput, calls=%fused_computation.15 | convolution fusion | flops 439746560 | bytes 3936768 | tf_op jit(solution)/shard_map/iak,ikl->ial/dot_general | solution.py:98
  58.9 1.3 collective-permute-start
  60.2 3.6 %collective-permute-start.1 = (bf16[6,128,128]{2,1,0:T(8,128)(2,1)S(1)}, bf16[6,128,128]{2,1,0:T(8,128)(2,1)S(1)}, u32[]{:S(2)}, u32[]{:S(2)}) collective-permute-start(bf16[6,128,128]{2,1,0:T(8,128)(2,1)S(1)} %get-tuple-element.10), channel_id=1, source_target_pairs={{1,0},{2,1},{3,2},{4,3},{5,4},{6,5},{7,6},{8,7},{9,8},{10,9},{11,1... | collective-permute-start | bytes 589832 | tf_op jit(solution)/shard_map/ppermute | solution.py:22
  64.5 4.0 %collective-permute-done = bf16[6,128,128]{2,1,0:T(8,128)(2,1)S(1)} collective-permute-done((bf16[6,128,128]{2,1,0:T(8,128)(2,1)S(1)}, bf16[6,128,128]{2,1,0:T(8,128)(2,1)S(1)}, u32[]{:S(2)}, u32[]{:S(2)}) %collective-permute-start) | collective-permute-done | bytes 196640 | tf_op jit(solution)/shard_map/ppermute | solution.py:20
  68.6 1.4 bitcast_select_fusion.1.right_ref
  70.0 25.6 %all-gather.5.cloned.1.call-done.left_ref = bf16[8,128,1664]{2,1,0:T(8,128)(2,1)} async-done(((bf16[8,8,1664]{2,1,0:T(8,128)(2,1)}), bf16[8,128,1664]{2,1,0:T(8,128)(2,1)}) %all-gather.5.cloned.1.call-update) | async-done | bytes 3407888 | tf_op jit(solution)/shard_map/all_gather | solution.py:88
  95.6 7.1 %shard_map.37 = bf16[8,128,128]{2,1,0:T(8,128)(2,1)} custom-call(bf16[8,128,1664]{2,1,0:T(8,128)(2,1)} %all-gather.5.cloned.1.call-done.left_ref, bf16[2560,256]{1,0:T(8,128)(2,1)} %bitcast_select_fusion.1.right_ref, f32[8,1,256]{2,1,0:T(1,128)} %reshape.441.keep_ref, f32[8,1,128]{2,1,0:T(1,128)} %compare_select_fusion.rest_0_, f32[128,128]{1,0:T(8,128)} %fusion.27.rest_1_), custom_call_target="tpu_custom_call" | custom-call | flops 872415232 | bytes 4718592 | tf_op jit(solution)/shard_map/pallas_call | solution.py:57
  102.7 1.0 fusion.57
  103.7 1.3 collective-permute-start.2
  105.0 3.6 %collective-permute-start.3 = (bf16[6,128,128]{2,1,0:T(8,128)(2,1)S(1)}, bf16[6,128,128]{2,1,0:T(8,128)(2,1)S(1)}, u32[]{:S(2)}, u32[]{:S(2)}) collective-permute-start(bf16[6,128,128]{2,1,0:T(8,128)(2,1)S(1)} %get-tuple-element.8), channel_id=1, source_target_pairs={{1,0},{2,1},{3,2},{4,3},{5,4},{6,5},{7,6},{8,7},{9,8},{10,9},{11,1... | collective-permute-start | bytes 589832 | tf_op jit(solution)/shard_map/ppermute | solution.py:22
  108.6 4.7 %collective-permute-done.2 = bf16[6,128,128]{2,1,0:T(8,128)(2,1)S(1)} collective-permute-done((bf16[6,128,128]{2,1,0:T(8,128)(2,1)S(1)}, bf16[6,128,128]{2,1,0:T(8,128)(2,1)S(1)}, u32[]{:S(2)}, u32[]{:S(2)}) %collective-permute-start.2) | collective-permute-done | bytes 196640 | tf_op jit(solution)/shard_map/ppermute | solution.py:20
  113.3 1.0 pad_maximum_fusion.1
  114.3 1.4 bitcast_select_fusion.right_ref
  115.7 7.0 %shard_map.38 = bf16[8,128,128]{2,1,0:T(8,128)(2,1)} custom-call(bf16[8,128,1664]{2,1,0:T(8,128)(2,1)} %all-gather.3.cloned.1.call-done.left_ref, bf16[2560,256]{1,0:T(8,128)(2,1)} %bitcast_select_fusion.right_ref, f32[8,1,256]{2,1,0:T(1,128)} %reshape.441.keep_ref), custom_call_target="tpu_custom_call" | custom-call | flops 872415232 | bytes 4718592 | tf_op jit(solution)/shard_map/pallas_call | solution.py:57
  122.7 1.7 %copy_bitcast_fusion = bf16[16,8,8,128]{3,2,1,0:T(8,128)(2,1)} fusion(bf16[8,128,128]{2,1,0:T(8,128)(2,1)} %shard_map.38), kind=kLoop, calls=%fused_computation.29 | loop fusion | bytes 524288 | tf_op jit(solution)/shard_map/transpose | solution.py:124
  124.4 5.6 %all-to-all-start = ((bf16[16,8,8,128]{3,2,1,0:T(8,128)(2,1)}), bf16[16,8,8,128]{3,2,1,0:T(8,128)(2,1)S(1)}, u32[]{:S(2)}, u32[]{:S(2)}) async-start(bf16[16,8,8,128]{3,2,1,0:T(8,128)(2,1)} %copy_bitcast_fusion), calls=%async_computation | async-start | bytes 524288 | tf_op jit(solution)/shard_map/all_to_all | solution.py:125
  130.5 9.2 %all-to-all-done = bf16[16,8,8,128]{3,2,1,0:T(8,128)(2,1)S(1)} async-done(((bf16[16,8,8,128]{3,2,1,0:T(8,128)(2,1)}), bf16[16,8,8,128]{3,2,1,0:T(8,128)(2,1)S(1)}, u32[]{:S(2)}, u32[]{:S(2)}) %all-to-all-start) | async-done | bytes 262176 | tf_op jit(solution)/shard_map/all_to_all | solution.py:125
  139.7 3.1 %fusion.15 = bf16[8,8,16,128]{3,1,2,0:T(8,128)(2,1)S(1)} fusion(pred[128,2048]{1,0:T(8,128)(4,1)S(1)} %get-tuple-element.15, pred[128,2048]{1,0:T(8,128)(4,1)S(1)} %get-tuple-element.16, pred[16,2048]{1,0:T(8,128)(4,1)S(1)} %iota_compare_fusion, bf16[16,8,8,128]{3,2,1,0:T(8,128)(2,1)S(1)} %all-to-all-done), kind=kOutput, calls=%fused_computation.19 | convolution fusion | flops 545390592 | bytes 1081344 | tf_op jit(solution)/shard_map/pml,pln->mn/dot_general | solution.py:133
  (38 shorter events, 4.5 us)
Async XLA Ops:
  6.5 1.7 %copy-start = (bf16[8,12,8,128]{3,2,1,0:T(8,128)(2,1)S(1)}, bf16[8,12,8,128]{3,2,1,0:T(8,128)(2,1)}, u32[]{:S(2)}) copy-start(bf16[8,12,8,128]{3,2,1,0:T(8,128)(2,1)} %param.4) | copy-start | bytes 589828
  6.5 47.8 %all-gather.3.cloned.1.call-start = ((), (), s32[]{:S(2)}) async-start(), calls=%async_computation.1 | async-start | bytes 3620864 | tf_op jit(solution)/shard_map/all_gather | solution.py:87
  9.3 86.2 %all-gather.5.cloned.1.call-start = ((), (), s32[]{:S(2)}) async-start(), calls=%async_computation.2 | async-start | bytes 3620864 | tf_op jit(solution)/shard_map/all_gather | solution.py:88
  58.9 9.6 %collective-permute-start = (bf16[6,128,128]{2,1,0:T(8,128)(2,1)S(1)}, bf16[6,128,128]{2,1,0:T(8,128)(2,1)S(1)}, u32[]{:S(2)}, u32[]{:S(2)}) collective-permute-start(bf16[6,128,128]{2,1,0:T(8,128)(2,1)S(1)} %get-tuple-element.9), channel_id=1, source_target_pairs={{0,1},{1,2},{2,3},{3,4},{4,5},{5,6},{6,7},{7,8},{8,9},{9,10},{10,1... | collective-permute-start | bytes 589832 | tf_op jit(solution)/shard_map/ppermute | solution.py:20
  60.2 8.3 %collective-permute-start.1 = (bf16[6,128,128]{2,1,0:T(8,128)(2,1)S(1)}, bf16[6,128,128]{2,1,0:T(8,128)(2,1)S(1)}, u32[]{:S(2)}, u32[]{:S(2)}) collective-permute-start(bf16[6,128,128]{2,1,0:T(8,128)(2,1)S(1)} %get-tuple-element.10), channel_id=1, source_target_pairs={{1,0},{2,1},{3,2},{4,3},{5,4},{6,5},{7,6},{8,7},{9,8},{10,9},{11,1... | collective-permute-start | bytes 589832 | tf_op jit(solution)/shard_map/ppermute | solution.py:22
  103.7 9.6 %collective-permute-start.2 = (bf16[6,128,128]{2,1,0:T(8,128)(2,1)S(1)}, bf16[6,128,128]{2,1,0:T(8,128)(2,1)S(1)}, u32[]{:S(2)}, u32[]{:S(2)}) collective-permute-start(bf16[6,128,128]{2,1,0:T(8,128)(2,1)S(1)} %get-tuple-element.7), channel_id=1, source_target_pairs={{0,1},{1,2},{2,3},{3,4},{4,5},{5,6},{6,7},{7,8},{8,9},{9,10},{10,1... | collective-permute-start | bytes 589832 | tf_op jit(solution)/shard_map/ppermute | solution.py:20
  105.0 8.3 %collective-permute-start.3 = (bf16[6,128,128]{2,1,0:T(8,128)(2,1)S(1)}, bf16[6,128,128]{2,1,0:T(8,128)(2,1)S(1)}, u32[]{:S(2)}, u32[]{:S(2)}) collective-permute-start(bf16[6,128,128]{2,1,0:T(8,128)(2,1)S(1)} %get-tuple-element.8), channel_id=1, source_target_pairs={{1,0},{2,1},{3,2},{4,3},{5,4},{6,5},{7,6},{8,7},{9,8},{10,9},{11,1... | collective-permute-start | bytes 589832 | tf_op jit(solution)/shard_map/ppermute | solution.py:22
  124.4 15.3 %all-to-all-start = ((bf16[16,8,8,128]{3,2,1,0:T(8,128)(2,1)}), bf16[16,8,8,128]{3,2,1,0:T(8,128)(2,1)S(1)}, u32[]{:S(2)}, u32[]{:S(2)}) async-start(bf16[16,8,8,128]{3,2,1,0:T(8,128)(2,1)} %copy_bitcast_fusion), calls=%async_computation | async-start | bytes 524288 | tf_op jit(solution)/shard_map/all_to_all | solution.py:125
Sparse Core Ops, SparseCore 0:
  9.4 44.8 all-gather.2
  56.1 39.3 all-gather.4

commit v2 on v1

--- a/solution.py
+++ b/solution.py
@@ -11,6 +11,103 @@
 REACH = 2 * HALO + 1
 FOLD = 16
 SPLIT = ("row", "col")
+
+MESH = pl.DeviceIdType.MESH
+
+
+def gather_kernel(z_ref, y_ref, z_out, y_out, send, recv, pair_send, pair_recv, own):
+    core, chip, chips = lax.axis_index("row"), lax.axis_index("col"), lax.axis_size("col")
+    part = z_ref.shape[1]
+    other = 1 - core
+    ahead, behind = lax.rem(chip + 1, chips), lax.rem(chip + chips - 1, chips)
+    targets = (ahead, behind)
+    ins, outs = (z_ref, y_ref), (z_out, y_out)
+
+    barrier = pltpu.get_barrier_semaphore()
+    pl.semaphore_signal(barrier, inc=1, device_id={"col": ahead}, device_id_type=MESH)
+    pl.semaphore_signal(barrier, inc=1, device_id={"col": behind}, device_id_type=MESH)
+    pl.semaphore_signal(barrier, inc=1, device_id={"row": other}, device_id_type=MESH)
+    pl.semaphore_wait(barrier, 3)
+
+    def place(which, at):
+        at = lax.rem(at + 2 * chips, chips)
+        first = pl.multiple_of((core * chips + at) * part, part)
+        return outs[which].at[:, pl.ds(first, part), :]
+
+    def pass_on(which, way, step):
+        at = chip - step if way == 0 else chip + step
+        there = place(which, at)
+        return pltpu.make_async_remote_copy(
+            src_ref=ins[which] if step == 0 else there,
+            dst_ref=there,
+            send_sem=send.at[which, way, step],
+            recv_sem=recv.at[which, way, step],
+            device_id={"col": targets[way]},
+            device_id_type=MESH,
+        )
+
+    def share(which, slot, source, at):
+        return pltpu.make_async_remote_copy(
+            src_ref=source,
+            dst_ref=place(which, at),
+            send_sem=pair_send.at[which, slot],
+            recv_sem=pair_recv.at[which, slot],
+            device_id={"row": other},
+            device_id_type=MESH,
+        )
+
+    steps = lambda which, way: chips // 2 - (1 if which != way else 0)
+    arms = [(which, way) for which in range(2) for way in range(2)]
+    started, waiting, kept = {}, [], []
+    for which, way in arms:
+        started[which, way] = pass_on(which, way, 0)
+        started[which, way].start()
+        waiting.append(started[which, way])
+    for which in range(2):
+        shared = share(which, 0, ins[which], chip)
+        shared.start()
+        kept.append(shared)
+        mine = pltpu.make_async_copy(ins[which], place(which, chip), own.at[which])
+        mine.start()
+        kept.append(mine)
+    for step in range(1, chips // 2 + 1):
+        for which, way in arms:
+            if step > steps(which, way):
+                continue
+            started[which, way].wait_recv()
+            if step < steps(which, way):
+                started[which, way] = pass_on(which, way, step)
+                started[which, way].start()
+                waiting.append(started[which, way])
+            at = chip - step if way == 0 else chip + step
+            slot = step if way == 0 else chips // 2 + step
+            shared = share(which, slot, place(which, at), at)
+            shared.start()
+            kept.append(shared)
+    for copy in waiting:
+        copy.wait_send()
+    for copy in kept:
+        copy.wait()
+
+
+def gathered(z_mine, y_mine, parts):
+    rows, part, depth = z_mine.shape
+    whole = jax.ShapeDtypeStruct((rows, parts * part, depth), z_mine.dtype)
+    half = lax.axis_size("col") // 2
+    return pl.pallas_call(
+        gather_kernel,
+        out_shape=(whole, whole),
+        in_specs=[pl.BlockSpec(memory_space=pltpu.VMEM)] * 2,
+        out_specs=(pl.BlockSpec(memory_space=pl.ANY), pl.BlockSpec(memory_space=pl.ANY)),
+        scratch_shapes=[
+            pltpu.SemaphoreType.DMA((2, 2, half)),
+            pltpu.SemaphoreType.DMA((2, 2, half)),
+            pltpu.SemaphoreType.DMA((2, 2 * half + 1)),
+            pltpu.SemaphoreType.DMA((2, 2 * half + 1)),
+            pltpu.SemaphoreType.DMA((2,)),
+        ],
+        compiler_params=pltpu.CompilerParams(collective_id=0, has_side_effects=True),
+    )(z_mine, y_mine)
 
 
 def halo_rows(rows):
@@ -84,8 +181,7 @@
         spread = spread.astype(jnp.bfloat16).transpose(1, 2, 0, 3)
         return spread.reshape(rows, part, REACH * block)
 
-    z_left = lax.all_gather(dense(z_blocks), SPLIT, axis=1, tiled=True)
-    y_left = lax.all_gather(dense(y_blocks), SPLIT, axis=1, tiled=True)
+    z_left, y_left = gathered(dense(z_blocks), dense(y_blocks), parts)
 
     lane = jnp.arange(FOLD * part, dtype=jnp.int32)
     lane_col, lane_in = lane // part, lane % part

time: 151 us -> 116 us (0.77)
  waiting for transfers between devices: 84.5 us -> 16.1 us
  Pallas kernels: 14.1 us -> 59.7 us
  between operations: 13.5 us -> 0.16 us
    all_gather x2 -> x0, waiting for transfers between devices: 66.6 us -> none  [the longest x1 41 us: local(): z_left = lax.all_gather(dense(z_blocks), SPLIT, axis=1, tiled=True)]
    pallas_call x0 -> x1, Pallas kernels: none -> 45.6 us  [gathered(): pl.pallas_call(gather_kernel, out_shape=(whole, whole), in_specs=[pl.Bloc...]
    ppermute x2, waiting for transfers between devices: 8.74 us -> 6.88 us  [halo_rows(): lax.ppermute(rows[-HALO:], 'cuts', [(i, (i + 1) % count) for i in range(c...]
  transfers between devices with their start and end apart: 7 -> 5, of which waited for: 5 -> 3; matrix products, arithmetic and copies ran while one was open for 7% -> 2% of each run, Pallas kernels for 0% -> 0%
where the time goes in v2:
time: 116 us; the launch traced here: 115 us
  Pallas kernels  59.7 us (51%)
  waiting for transfers between devices  16.1 us (14%)
  starting transfers between devices  16 us (14%)
  matrix products  9.25 us (8%)
  other arithmetic  7.75 us (7%)
  local copies, waits for them, and re-layouts  6.03 us (5%)
    pallas_call x1, Pallas kernels, gathered(): pl.pallas_call(gather_kernel, out_shape=(whole, whole), in_specs=[pl.Bloc...  45.6 us
    pallas_call x2, Pallas kernels, banded_product(): pl.pallas_call(functools.partial(product_kernel, bool(diagonal)), grid=(r...  14.1 us
    all_to_all x1, waiting for transfers between devices, local(): got = lax.all_to_all(sent, SPLIT, 0, 0, tiled=True)  9.2 us
    ppermute x2, starting transfers between devices, halo_rows(): lax.ppermute(rows[:HALO], 'cuts', [((i + 1) % count, i) for i in range(co...  8.58 us
    ppermute x2, waiting for transfers between devices, halo_rows(): lax.ppermute(rows[-HALO:], 'cuts', [(i, (i + 1) % count) for i in range(c...  6.88 us
    all_to_all x1, starting transfers between devices, local(): got = lax.all_to_all(sent, SPLIT, 0, 0, tiled=True)  6.09 us
    dot_general x1, matrix products, local(): jnp.einsum('iak,ikl->ial', z_left, chooser, preferred_element_type=jnp.fl...  4.54 us
    dot_general x1, matrix products, local(): jnp.einsum('pml,pln->mn', got, mover, preferred_element_type=jnp.float32)  3.08 us
  transfers between devices with their start and end apart: 5, of which 3 were waited for; matrix products, arithmetic and copies ran while one was open for 2% of the time, Pallas kernels for 0%

profile of v2, /device:TPU:1, one launch (start us, length us, event | category | flops | bytes accessed | tf_op | source)
XLA Modules:
  0.0 115.1 jit_solution(10236653451690428063)
XLA Ops:
  0.0 0.8 add_select_fusion.11
  0.9 0.8 add_select_fusion.8
  2.0 0.9 reshape.436.z_ref
  2.8 1.1 fusion.17
  3.9 0.9 reshape.437.y_ref
  4.9 45.6 %shard_map.37 = (bf16[8,128,1664]{2,1,0:T(8,128)(2,1)}, bf16[8,128,1664]{2,1,0:T(8,128)(2,1)}) custom-call(bf16[8,8,1664]{2,1,0:T(8,128)(2,1)} %reshape.436.z_ref, bf16[8,8,1664]{2,1,0:T(8,128)(2,1)} %reshape.437.y_ref), custom_call_target="tpu_custom_call" | custom-call | tf_op jit(solution)/shard_map/pallas_call | solution.py:97
  50.8 4.5 %fusion.12 = bf16[8,128,128]{2,1,0:T(8,128)(2,1)S(1)} fusion(bf16[8,128,1664]{2,1,0:T(8,128)(2,1)} %get-tuple-element.7.left_ref, s32[128]{0:T(128)S(1)} %and_select_fusion.3, s32[8,1664]{1,0:T(8,128)S(1)} %add_select_fusion, pred[1664,128]{1,0:T(8,128)(4,1)S(1)} %broadcast_compare_fusion.2), kind=kOutput, calls=%fused_computation.15 | convolution fusion | flops 439746560 | bytes 3936768 | tf_op jit(solution)/shard_map/iak,ikl->ial/dot_general | solution.py:194
  55.5 1.3 %collective-permute-start = (bf16[6,128,128]{2,1,0:T(8,128)(2,1)S(1)}, bf16[6,128,128]{2,1,0:T(8,128)(2,1)S(1)}, u32[]{:S(2)}, u32[]{:S(2)}) collective-permute-start(bf16[6,128,128]{2,1,0:T(8,128)(2,1)S(1)} %get-tuple-element.13), channel_id=1, source_target_pairs={{0,1},{1,2},{2,3},{3,4},{4,5},{5,6},{6,7},{7,8},{8,9},{9,10},{10,1... | collective-permute-start | bytes 589832 | tf_op jit(solution)/shard_map/ppermute | solution.py:117
  56.7 3.8 %collective-permute-start.1 = (bf16[6,128,128]{2,1,0:T(8,128)(2,1)S(1)}, bf16[6,128,128]{2,1,0:T(8,128)(2,1)S(1)}, u32[]{:S(2)}, u32[]{:S(2)}) collective-permute-start(bf16[6,128,128]{2,1,0:T(8,128)(2,1)S(1)} %get-tuple-element.14), channel_id=1, source_target_pairs={{1,0},{2,1},{3,2},{4,3},{5,4},{6,5},{7,6},{8,7},{9,8},{10,9},{11,1... | collective-permute-start | bytes 589832 | tf_op jit(solution)/shard_map/ppermute | solution.py:119
  62.1 0.7 compare_select_fusion.rest_0_
  62.7 2.7 %collective-permute-done = bf16[6,128,128]{2,1,0:T(8,128)(2,1)S(1)} collective-permute-done((bf16[6,128,128]{2,1,0:T(8,128)(2,1)S(1)}, bf16[6,128,128]{2,1,0:T(8,128)(2,1)S(1)}, u32[]{:S(2)}, u32[]{:S(2)}) %collective-permute-start) | collective-permute-done | bytes 196640 | tf_op jit(solution)/shard_map/ppermute | solution.py:117
  65.6 1.4 %bitcast_select_fusion.1.right_ref = bf16[2560,256]{1,0:T(8,128)(2,1)} fusion(bf16[2560,128]{1,0:T(8,128)(2,1)S(1)} %bitcast.38, pred[20,256]{1,0:T(8,128)(4,1)S(1)} %pad_add_fusion), kind=kLoop, calls=%fused_computation.9 | loop fusion | flops 3276800 | bytes 1971200 | tf_op jit(solution)/shard_map/jit(_where)/select_n | solution.py:207
  66.9 7.1 %shard_map.38 = bf16[8,128,128]{2,1,0:T(8,128)(2,1)} custom-call(bf16[8,128,1664]{2,1,0:T(8,128)(2,1)} %get-tuple-element.8.left_ref, bf16[2560,256]{1,0:T(8,128)(2,1)} %bitcast_select_fusion.1.right_ref, f32[8,1,256]{2,1,0:T(1,128)} %reshape.441.keep_ref, f32[8,1,128]{2,1,0:T(1,128)} %compare_select_fusion.rest_0_, f32[128,128]{1,0:T(8,128)} %fusion.27.rest_1_), custom_call_target="tpu_custom_call" | custom-call | flops 872415232 | bytes 4718592 | tf_op jit(solution)/shard_map/pallas_call | solution.py:154
  74.0 1.0 fusion.57
  75.2 4.8 %collective-permute-start.3 = (bf16[6,128,128]{2,1,0:T(8,128)(2,1)S(1)}, bf16[6,128,128]{2,1,0:T(8,128)(2,1)S(1)}, u32[]{:S(2)}, u32[]{:S(2)}) collective-permute-start(bf16[6,128,128]{2,1,0:T(8,128)(2,1)S(1)} %get-tuple-element.12), channel_id=1, source_target_pairs={{1,0},{2,1},{3,2},{4,3},{5,4},{6,5},{7,6},{8,7},{9,8},{10,9},{11,1... | collective-permute-start | bytes 589832 | tf_op jit(solution)/shard_map/ppermute | solution.py:119
  79.9 4.1 %collective-permute-done.2 = bf16[6,128,128]{2,1,0:T(8,128)(2,1)S(1)} collective-permute-done((bf16[6,128,128]{2,1,0:T(8,128)(2,1)S(1)}, bf16[6,128,128]{2,1,0:T(8,128)(2,1)S(1)}, u32[]{:S(2)}, u32[]{:S(2)}) %collective-permute-start.2) | collective-permute-done | bytes 196640 | tf_op jit(solution)/shard_map/ppermute | solution.py:117
  84.1 1.0 pad_maximum_fusion.1
  85.1 1.4 %bitcast_select_fusion.right_ref = bf16[2560,256]{1,0:T(8,128)(2,1)} fusion(bf16[2560,128]{1,0:T(8,128)(2,1)S(1)} %bitcast.37, pred[20,256]{1,0:T(8,128)(4,1)S(1)} %pad_add_fusion), kind=kLoop, calls=%fused_computation.8 | loop fusion | flops 3276800 | bytes 1971200 | tf_op jit(solution)/shard_map/jit(_where)/select_n | solution.py:207
  86.5 7.0 %shard_map.39 = bf16[8,128,128]{2,1,0:T(8,128)(2,1)} custom-call(bf16[8,128,1664]{2,1,0:T(8,128)(2,1)} %get-tuple-element.7.left_ref, bf16[2560,256]{1,0:T(8,128)(2,1)} %bitcast_select_fusion.right_ref, f32[8,1,256]{2,1,0:T(1,128)} %reshape.441.keep_ref), custom_call_target="tpu_custom_call" | custom-call | flops 872415232 | bytes 4718592 | tf_op jit(solution)/shard_map/pallas_call | solution.py:154
  93.5 1.7 %copy_bitcast_fusion = bf16[16,8,8,128]{3,2,1,0:T(8,128)(2,1)} fusion(bf16[8,128,128]{2,1,0:T(8,128)(2,1)} %shard_map.39), kind=kLoop, calls=%fused_computation.29 | loop fusion | bytes 524288 | tf_op jit(solution)/shard_map/transpose | solution.py:220
  95.2 6.1 %all-to-all-start = ((bf16[16,8,8,128]{3,2,1,0:T(8,128)(2,1)}), bf16[16,8,8,128]{3,2,1,0:T(8,128)(2,1)S(1)}, u32[]{:S(2)}, u32[]{:S(2)}) async-start(bf16[16,8,8,128]{3,2,1,0:T(8,128)(2,1)} %copy_bitcast_fusion), calls=%async_computation | async-start | bytes 524288 | tf_op jit(solution)/shard_map/all_to_all | solution.py:221
  101.8 9.2 %all-to-all-done = bf16[16,8,8,128]{3,2,1,0:T(8,128)(2,1)S(1)} async-done(((bf16[16,8,8,128]{3,2,1,0:T(8,128)(2,1)}), bf16[16,8,8,128]{3,2,1,0:T(8,128)(2,1)S(1)}, u32[]{:S(2)}, u32[]{:S(2)}) %all-to-all-start) | async-done | bytes 262176 | tf_op jit(solution)/shard_map/all_to_all | solution.py:221
  111.0 3.1 %fusion.15 = bf16[8,8,16,128]{3,1,2,0:T(8,128)(2,1)S(1)} fusion(pred[128,2048]{1,0:T(8,128)(4,1)S(1)} %get-tuple-element.19, pred[128,2048]{1,0:T(8,128)(4,1)S(1)} %get-tuple-element.20, pred[16,2048]{1,0:T(8,128)(4,1)S(1)} %iota_compare_fusion, bf16[16,8,8,128]{3,2,1,0:T(8,128)(2,1)S(1)} %all-to-all-done), kind=kOutput, calls=%fused_computation.19 | convolution fusion | flops 545390592 | bytes 1081344 | tf_op jit(solution)/shard_map/pml,pln->mn/dot_general | solution.py:229
  114.3 0.7 copy.34
  (33 shorter events, 3.1 us)
Async XLA Ops:
  0.0 1.7 %copy-start = (bf16[8,12,8,128]{3,2,1,0:T(8,128)(2,1)S(1)}, bf16[8,12,8,128]{3,2,1,0:T(8,128)(2,1)}, u32[]{:S(2)}) copy-start(bf16[8,12,8,128]{3,2,1,0:T(8,128)(2,1)} %param.4) | copy-start | bytes 589828
  55.5 10.0 %collective-permute-start = (bf16[6,128,128]{2,1,0:T(8,128)(2,1)S(1)}, bf16[6,128,128]{2,1,0:T(8,128)(2,1)S(1)}, u32[]{:S(2)}, u32[]{:S(2)}) collective-permute-start(bf16[6,128,128]{2,1,0:T(8,128)(2,1)S(1)} %get-tuple-element.13), channel_id=1, source_target_pairs={{0,1},{1,2},{2,3},{3,4},{4,5},{5,6},{6,7},{7,8},{8,9},{9,10},{10,1... | collective-permute-start | bytes 589832 | tf_op jit(solution)/shard_map/ppermute | solution.py:117
  56.7 8.7 %collective-permute-start.1 = (bf16[6,128,128]{2,1,0:T(8,128)(2,1)S(1)}, bf16[6,128,128]{2,1,0:T(8,128)(2,1)S(1)}, u32[]{:S(2)}, u32[]{:S(2)}) collective-permute-start(bf16[6,128,128]{2,1,0:T(8,128)(2,1)S(1)} %get-tuple-element.14), channel_id=1, source_target_pairs={{1,0},{2,1},{3,2},{4,3},{5,4},{6,5},{7,6},{8,7},{9,8},{10,9},{11,1... | collective-permute-start | bytes 589832 | tf_op jit(solution)/shard_map/ppermute | solution.py:119
  75.1 9.0 %collective-permute-start.2 = (bf16[6,128,128]{2,1,0:T(8,128)(2,1)S(1)}, bf16[6,128,128]{2,1,0:T(8,128)(2,1)S(1)}, u32[]{:S(2)}, u32[]{:S(2)}) collective-permute-start(bf16[6,128,128]{2,1,0:T(8,128)(2,1)S(1)} %get-tuple-element.11), channel_id=1, source_target_pairs={{0,1},{1,2},{2,3},{3,4},{4,5},{5,6},{6,7},{7,8},{8,9},{9,10},{10,1... | collective-permute-start | bytes 589832 | tf_op jit(solution)/shard_map/ppermute | solution.py:117
  75.2 8.9 %collective-permute-start.3 = (bf16[6,128,128]{2,1,0:T(8,128)(2,1)S(1)}, bf16[6,128,128]{2,1,0:T(8,128)(2,1)S(1)}, u32[]{:S(2)}, u32[]{:S(2)}) collective-permute-start(bf16[6,128,128]{2,1,0:T(8,128)(2,1)S(1)} %get-tuple-element.12), channel_id=1, source_target_pairs={{1,0},{2,1},{3,2},{4,3},{5,4},{6,5},{7,6},{8,7},{9,8},{10,9},{11,1... | collective-permute-start | bytes 589832 | tf_op jit(solution)/shard_map/ppermute | solution.py:119
  95.2 15.7 %all-to-all-start = ((bf16[16,8,8,128]{3,2,1,0:T(8,128)(2,1)}), bf16[16,8,8,128]{3,2,1,0:T(8,128)(2,1)S(1)}, u32[]{:S(2)}, u32[]{:S(2)}) async-start(bf16[16,8,8,128]{3,2,1,0:T(8,128)(2,1)} %copy_bitcast_fusion), calls=%async_computation | async-start | bytes 524288 | tf_op jit(solution)/shard_map/all_to_all | solution.py:221
